TPU v7x, 32 devices: a whole 2x2x4 slice. The times are simulated.
32 devices in a mesh: grp: 2 (over x), ctg: 16 (over z, y, core).
Axes of the slice: x: 2, y: 2, z: 4, core: 2. Of those that a mesh axis runs over, the one named last changes fastest.
Arguments:
- flow_tiles: bfloat16 [128, 256, 3072], P('ctg'), may hold values from -0.109375 to 0.109375
- tile_pattern: int32 [128, 2, 24], P('ctg'), may hold values 0 or 1
- monitored: int32 [128, 256], P('ctg'), may hold values from 0 to 16383
- ratings: float32 [16384], replicated, may hold values from 0.3 to 3
- base_flow: float32 [64, 128, 256], P('grp', 'ctg'), parts along dimension 0, may hold values from -6 to 6
- unit_cost: float32 [64, 3072], P(('grp', 'ctg')), parts along dimension 0, may hold values from -6 to 6
- unit_floor: float32 [3072], replicated, may hold values from 0 to 0.5
- unit_span: float32 [3072], replicated, may hold values from 0.5 to 2
- ramp_limit: float32 [3072], replicated, may hold values from 0.05 to 0.5
- ramp_mask: int32 [3072], replicated, may hold values 0 or 1
- demand: float32 [64], P(('grp', 'ctg')), parts along dimension 0, may hold values from 1228.8 to 2457.6
- start_output: float32 [64, 3072], P(('grp', 'ctg')), parts along dimension 0, may hold values from 0 to 1.5
- start_flow_dual: float32 [64, 128, 256], P('grp', 'ctg'), parts along dimension 0, may hold values from -2 to 2
- start_ramp_dual: float32 [64, 3072], P(('grp', 'ctg')), parts along dimension 0, may hold values from -3 to 3
Outputs:
- output_levels: float32 [64, 3072], P(('grp', 'ctg')), parts along dimension 0
- flow_dual: float32 [64, 128, 256], P('grp', 'ctg'), parts along dimension 0
- ramp_dual: float32 [64, 3072], P(('grp', 'ctg')), parts along dimension 0
- balance_price: float32 [64], P(('grp', 'ctg')), parts along dimension 0
There are 2 independent parts, one for each index of `grp`. A program takes and returns all parts, laid end to end along the dimension named above; an argument that names none is the same for every part. Nothing has to cross between parts.
All inputs are finite; a program needn't handle non-finite values. No bound on the sum of `tile_pattern` on one device may be relied on, other than what follows from the above.
Results may differ from a plain program's by a relative error of at most 0.0045.
Values may be sent and summed in bfloat16 or wider, within the bound.
A program may use at most 128 MiB of HBM per device.

v0:
```python
import math
import jax
import jax.numpy as jnp
from jax import lax
from jax.sharding import PartitionSpec as P

ITERS = 4


def mask_tiles(flow_tiles, tile_pattern):
    ctg_count, line_count, unit_count = flow_tiles.shape
    blocks = flow_tiles.reshape(ctg_count, line_count // 128, 128, unit_count // 128, 128)
    gates = tile_pattern.astype(jnp.bfloat16)[:, :, None, :, None]
    return (blocks * gates).reshape(ctg_count, line_count, unit_count)


def dual_prox(trial, dual_step, lower_side, upper_side):
    return trial - dual_step * jnp.clip(trial / dual_step, lower_side, upper_side)


def body(
    flow_tiles,
    tile_pattern,
    monitored,
    ratings,
    base_flow,
    unit_cost,
    unit_floor,
    unit_span,
    ramp_limit,
    ramp_mask,
    demand,
    start_output,
    start_flow_dual,
    start_ramp_dual,
):
    ctg_count, line_count, unit_count = flow_tiles.shape
    devices = lax.axis_size("ctg")
    position = lax.axis_index("ctg")
    masked = mask_tiles(flow_tiles, tile_pattern)
    flow_limit = ratings[monitored]
    flow_lower = base_flow - flow_limit[None]
    flow_upper = base_flow + flow_limit[None]
    step_size = 0.5 / (2.0 + math.sqrt(ctg_count * devices * line_count / unit_count))
    balance = 1.0 / math.sqrt(unit_count)
    ceiling = unit_floor + unit_span
    ramp_on = ramp_mask.astype(jnp.float32)
    weight = jnp.float32(1.0)
    hour_rows = start_output.shape[0]
    zero_row = jnp.zeros((1, unit_count), jnp.float32)
    flow_dual = start_flow_dual
    levels, costs, ramp_dual, demands = (
        lax.all_gather(start_output, "ctg", axis=0, tiled=True),
        lax.all_gather(unit_cost, "ctg", axis=0, tiled=True),
        lax.all_gather(start_ramp_dual, "ctg", axis=0, tiled=True),
        lax.all_gather(demand, "ctg", axis=0, tiled=True),
    )
    balance_price = jnp.zeros(demands.shape, jnp.float32)
    for iteration in range(ITERS):
        primal_step = step_size / weight
        dual_step = step_size * weight
        dual_half = flow_dual.astype(jnp.bfloat16)
        own_term = jnp.einsum("tkm,kmu->tu", dual_half, masked, preferred_element_type=jnp.float32)
        pulled = lax.psum(own_term.astype(jnp.bfloat16), "ctg").astype(jnp.float32)
        before = jnp.concatenate([zero_row, ramp_dual[:-1]], axis=0)
        gradient = (
            costs + pulled + ramp_on * (before - ramp_dual) + balance * balance_price[:, None]
        )
        moved = jnp.clip(levels - primal_step * gradient, unit_floor, ceiling)
        extended = 2.0 * moved - levels
        extended_half = extended.astype(jnp.bfloat16)
        flows = jnp.einsum("kmu,tu->tkm", masked, extended_half, preferred_element_type=jnp.float32)
        dual_new = dual_prox(flow_dual + dual_step * flows, dual_step, flow_lower, flow_upper)
        change = ramp_on * jnp.concatenate([extended[1:] - extended[:-1], zero_row], axis=0)
        ramp_new = dual_prox(ramp_dual + dual_step * change, dual_step, -ramp_limit, ramp_limit)
        balance_row = balance * (jnp.sum(extended, axis=1) - demands)
        price_new = balance_price + dual_step * balance_row
        if iteration < ITERS - 1:
            primal_sq = jnp.sum((moved - levels) ** 2)
            flow_sq = lax.psum(jnp.sum((dual_new - flow_dual) ** 2), "ctg")
            dual_sq = (
                flow_sq
                + jnp.sum((ramp_new - ramp_dual) ** 2)
                + jnp.sum((price_new - balance_price) ** 2)
            )
            weight = jnp.sqrt(weight) * ((dual_sq + 1e-06) / (primal_sq + 1e-06)) ** 0.25
        levels = moved
        flow_dual = dual_new
        ramp_dual = ramp_new
        balance_price = price_new
    first_hour = position * hour_rows
    own_levels = lax.dynamic_slice_in_dim(levels, first_hour, hour_rows, 0)
    own_ramp = lax.dynamic_slice_in_dim(ramp_dual, first_hour, hour_rows, 0)
    own_price = lax.dynamic_slice_in_dim(balance_price, first_hour, hour_rows, 0)
    return (own_levels, flow_dual, own_ramp, own_price)


def solution(mesh):
    return jax.shard_map(
        body,
        mesh=mesh,
        in_specs=(
            P("ctg", None, None),
            P("ctg", None, None),
            P("ctg", None),
            P(),
            P("grp", "ctg", None),
            P(("grp", "ctg"), None),
            P(),
            P(),
            P(),
            P(),
            P(("grp", "ctg")),
            P(("grp", "ctg"), None),
            P("grp", "ctg", None),
            P(("grp", "ctg"), None),
        ),
        out_specs=(
            P(("grp", "ctg"), None),
            P("grp", "ctg", None),
            P(("grp", "ctg"), None),
            P(("grp", "ctg")),
        ),
        check_vma=False,
    )
```

profile of v0, /device:TPU:0, one launch (start us, length us, event | category | flops | bytes accessed | tf_op | source)
XLA Modules:
  0.0 492.0 jit_solution(2523741557012118708)
XLA Ops:
  7.2 0.7 convert_element_type.57
  7.9 6.3 %mul.232 = bf16[8,2,128,24,128]{4,3,2,1,0:T(8,128)(2,1)} broadcast(bf16[8,2,24]{2,1,0:T(2,128)(2,1)S(1)} %convert_element_type.57), dimensions={0,1,3} | broadcast | bytes 12583680 | tf_op jit(solution)/shard_map/mul | solution.py:14
  14.2 19.3 %mul.233 = bf16[8,256,3072]{2,1,0:T(8,128)(2,1)} reshape(bf16[8,2,128,24,128]{4,3,2,1,0:T(8,128)(2,1)} %mul.232) | data formatting | bytes 25165824 | tf_op jit(solution)/shard_map/mul | solution.py:14
  33.5 11.4 %mul.234 = bf16[8,256,3072]{2,1,0:T(8,128)(2,1)S(1)} multiply(bf16[8,256,3072]{2,1,0:T(8,128)(2,1)} %param.14, bf16[8,256,3072]{2,1,0:T(8,128)(2,1)} %mul.233) | non-fusion elementwise | flops 6291456 | bytes 37748736 | tf_op jit(solution)/shard_map/mul | solution.py:14
  45.0 4.6 copy-done.1
  49.7 2.9 fusion.4
  52.6 0.0 all-reduce.17.cloned.1.call-start
  52.7 24.2 %all-gather.1 = f32[16,2,3072]{2,1,0:T(2,128)S(1)} all-gather(f32[1,2,3072]{2,1,0:T(2,128)S(1)} %bitcast.64), channel_id=1, replica_groups=mesh['grp'=2,'ctg'=16] {'ctg'}, dimensions={0}, use_global_device_ids=true | all-gather | bytes 417792 | tf_op jit(solution)/shard_map/all_gather | solution.py:54
  76.9 0.3 reshape.40
  77.2 18.6 %all-gather.2 = f32[16,2,3072]{2,1,0:T(2,128)S(1)} all-gather(f32[1,2,3072]{2,1,0:T(2,128)S(1)} %bitcast.65), channel_id=1, replica_groups=mesh['grp'=2,'ctg'=16] {'ctg'}, dimensions={0}, use_global_device_ids=true | all-gather | bytes 417792 | tf_op jit(solution)/shard_map/all_gather | solution.py:55
  95.8 0.3 reshape.42
  96.2 20.1 %all-gather = f32[16,2,3072]{2,1,0:T(2,128)S(1)} all-gather(f32[1,2,3072]{2,1,0:T(2,128)S(1)} %bitcast.66), channel_id=1, replica_groups=mesh['grp'=2,'ctg'=16] {'ctg'}, dimensions={0}, use_global_device_ids=true | all-gather | bytes 417792 | tf_op jit(solution)/shard_map/all_gather | solution.py:53
  116.3 0.3 reshape.38
  116.6 11.8 %gather_fusion = f32[2048]{0:T(1024)S(1)} fusion(f32[16384]{0:T(1024)S(1)} %copy-done, s32[2048]{0:T(1024)S(1)} %broadcast_clamp_fusion), kind=kCustom, calls=%fused_computation | custom fusion | bytes 24576 | tf_op jit(solution)/shard_map/gather | solution.py:41
  128.4 0.6 dynamic-slice
  129.7 0.2 dynamic-update-slice
  129.9 16.5 %all-reduce.15.cloned.1.call-done = bf16[32,3072]{1,0:T(8,128)(2,1)} async-done(((bf16[32,3072]{1,0:T(8,128)(2,1)}), bf16[32,3072]{1,0:T(8,128)(2,1)}) %all-reduce.15.cloned.1.call-update) | async-done | bytes 196624 | tf_op jit(solution)/shard_map/psum | solution.py:64
  146.5 1.7 multiply_reduce_fusion.4
  148.2 0.2 fusion.34
  148.4 9.1 %multiply_reduce_fusion.8 = (f32[]{:T(128)}, f32[32,8,256]{2,0,1:T(8,128)S(1)}) fusion(f32[32,8,256]{2,1,0:T(8,128)S(1)} %copy-done.3, f32[8,256]{1,0:T(8,128)S(1)} %reshape.25, f32[32,8,256]{2,1,0:T(8,128)S(1)} %copy-done.2, bf16[8,256,3072]{2,1,0:T(8,128)(2,1)} %copy-done.1, f32[32,3072]{1,0:T(8,128)S(1)} %get-tuple-element.42), kind=kOutput, calls=%fused_computation.47 | convolution fusion | flops 403537920 | bytes 13770756 | tf_op jit(solution)/shard_map/kmu,tu->tkm/dot_general | solution.py:72
  157.5 7.5 %fusion = bf16[32,3072]{1,0:T(8,128)(2,1)} fusion(bf16[8,256,3072]{2,1,0:T(8,128)(2,1)} %copy-done.1, f32[32,8,256]{2,0,1:T(8,128)S(1)} %get-tuple-element.46, f32[32,8,256]{2,1,0:T(8,128)S(1)} %copy-done.2, f32[8,256]{1,0:T(8,128)S(1)} %reshape.25), kind=kOutput, calls=%fused_computation.5 | convolution fusion | flops 403275776 | bytes 13312000 | tf_op jit(solution)/shard_map/tkm,kmu->tu/dot_general | solution.py:63
  165.0 0.0 all-reduce.19.cloned.1.call-start
  165.1 31.2 %all-reduce.9 = (f32[32]{0:T(128)S(1)}, f32[]{:T(128)}) all-reduce(f32[32]{0:T(128)S(1)} %dynamic-update-slice, f32[]{:T(128)} %get-tuple-element.45), channel_id=1, replica_groups=mesh['grp'=2,'ctg'=16] {'ctg'}, use_global_device_ids=true, to_apply=%add.8 | all-reduce | flops 33 | bytes 264
  196.2 0.8 multiply_reduce_fusion.5
  197.0 0.6 multiply_reduce_fusion.11
  200.3 54.7 %all-reduce.17.cloned.1.call-done = bf16[32,3072]{1,0:T(8,128)(2,1)} async-done(((bf16[32,3072]{1,0:T(8,128)(2,1)}), bf16[32,3072]{1,0:T(8,128)(2,1)}) %all-reduce.17.cloned.1.call-update) | async-done | bytes 196624 | tf_op jit(solution)/shard_map/psum | solution.py:64
  255.1 1.7 multiply_reduce_fusion.2
  256.8 0.2 fusion.33
  257.0 9.1 %multiply_reduce_fusion.7 = (f32[]{:T(128)}, f32[32,8,256]{2,0,1:T(8,128)S(1)}) fusion(f32[32,8,256]{2,0,1:T(8,128)S(1)} %get-tuple-element.46, f32[]{:T(128)S(6)} %mul.251, f32[8,256]{1,0:T(8,128)S(1)} %reshape.25, f32[32,8,256]{2,1,0:T(8,128)S(1)} %copy-done.2, bf16[8,256,3072]{2,1,0:T(8,128)(2,1)} %copy-done.1, f32[32,3072]{1,0:T(8,128)S(1)} %get-tuple-element.36), kind=kOutput, calls=%fused_computation.44 | convolution fusion | flops 403865600 | bytes 13770760 | tf_op jit(solution)/shard_map/kmu,tu->tkm/dot_general | solution.py:72
  266.1 0.8 multiply_reduce_fusion.3
  266.8 7.5 %fusion.1 = bf16[32,3072]{1,0:T(8,128)(2,1)} fusion(bf16[8,256,3072]{2,1,0:T(8,128)(2,1)} %copy-done.1, f32[32,8,256]{2,0,1:T(8,128)S(1)} %get-tuple-element.48, f32[]{:T(128)S(6)} %mul.251, f32[32,8,256]{2,1,0:T(8,128)S(1)} %copy-done.2, f32[8,256]{1,0:T(8,128)S(1)} %reshape.25), kind=kOutput, calls=%fused_computation.6 | convolution fusion | flops 403275776 | bytes 13312004 | tf_op jit(solution)/shard_map/tkm,kmu->tu/dot_general | solution.py:63
  274.3 0.0 all-reduce.21.cloned.1.call-start
  274.4 0.6 multiply_reduce_fusion.10
  275.0 31.3 %psum.52 = f32[]{:T(128)} all-reduce(f32[]{:T(128)} %get-tuple-element.47), channel_id=1, replica_groups=mesh['grp'=2,'ctg'=16] {'ctg'}, use_global_device_ids=true, to_apply=%region_9.10 | all-reduce | flops 1 | bytes 8 | tf_op jit(solution)/shard_map/psum | solution.py:80
  309.1 55.2 %all-reduce.19.cloned.1.call-done = bf16[32,3072]{1,0:T(8,128)(2,1)} async-done(((bf16[32,3072]{1,0:T(8,128)(2,1)}), bf16[32,3072]{1,0:T(8,128)(2,1)}) %all-reduce.19.cloned.1.call-update) | async-done | bytes 196624 | tf_op jit(solution)/shard_map/psum | solution.py:64
  364.3 1.7 multiply_reduce_fusion
  366.1 0.2 fusion.32
  366.3 9.1 %multiply_reduce_fusion.6 = (f32[]{:T(128)}, f32[32,8,256]{2,0,1:T(8,128)S(1)}) fusion(f32[32,8,256]{2,0,1:T(8,128)S(1)} %get-tuple-element.48, f32[]{:T(128)S(6)} %mul.268, f32[]{:T(128)S(6)} %mul.251, f32[8,256]{1,0:T(8,128)S(1)} %reshape.25, f32[32,8,256]{2,1,0:T(8,128)S(1)} %copy-done.2, bf16[8,256,3072]{2,1,0:T(8,128)(2,1)} %copy-done.1, ...), kind=kOutput, calls=%fused_computation.41 | convolution fusion | flops 403865600 | bytes 13770764 | tf_op jit(solution)/shard_map/kmu,tu->tkm/dot_general | solution.py:72
  375.3 0.8 multiply_reduce_fusion.1
  376.1 7.5 %fusion.2 = bf16[32,3072]{1,0:T(8,128)(2,1)} fusion(bf16[8,256,3072]{2,1,0:T(8,128)(2,1)} %copy-done.1, f32[32,8,256]{2,0,1:T(8,128)S(1)} %get-tuple-element.50, f32[]{:T(128)S(6)} %mul.268, f32[32,8,256]{2,1,0:T(8,128)S(1)} %copy-done.2, f32[8,256]{1,0:T(8,128)S(1)} %reshape.25), kind=kOutput, calls=%fused_computation.7 | convolution fusion | flops 403275776 | bytes 13312004 | tf_op jit(solution)/shard_map/tkm,kmu->tu/dot_general | solution.py:63
  383.6 0.6 multiply_reduce_fusion.9
  384.2 31.1 %psum.54 = f32[]{:T(128)} all-reduce(f32[]{:T(128)} %get-tuple-element.49), channel_id=1, replica_groups=mesh['grp'=2,'ctg'=16] {'ctg'}, use_global_device_ids=true, to_apply=%region_16.17 | all-reduce | flops 1 | bytes 8 | tf_op jit(solution)/shard_map/psum | solution.py:80
  418.0 55.5 %all-reduce.21.cloned.1.call-done = bf16[32,3072]{1,0:T(8,128)(2,1)} async-done(((bf16[32,3072]{1,0:T(8,128)(2,1)}), bf16[32,3072]{1,0:T(8,128)(2,1)}) %all-reduce.21.cloned.1.call-update) | async-done | bytes 196624 | tf_op jit(solution)/shard_map/psum | solution.py:64
  473.6 1.2 fusion.31
  474.9 8.4 %multiply_subtract_fusion.7 = f32[32,8,256]{2,0,1:T(8,128)S(1)} fusion(bf16[8,256,3072]{2,1,0:T(8,128)(2,1)} %copy-done.1, f32[32,8,256]{2,0,1:T(8,128)S(1)} %get-tuple-element.50, f32[32,3072]{1,0:T(8,128)S(1)} %get-tuple-element.19, f32[]{:T(128)S(6)} %mul.286, f32[]{:T(128)S(6)} %mul.268, f32[8,256]{1,0:T(8,128)S(1)} %reshape.25, ...), kind=kOutput, calls=%fused_computation.40 | convolution fusion | flops 403668992 | bytes 13770760 | tf_op jit(solution)/shard_map/kmu,tu->tkm/dot_general | solution.py:72
  483.3 0.9 copy.35
  484.2 0.6 dynamic_slice.11
  484.8 0.7 multiply_subtract_fusion.11
  (49 shorter events, 0.5 us)
Async XLA Ops:
  7.2 109.4 %copy-start = (f32[16384]{0:T(1024)S(1)}, f32[16384]{0:T(1024)}, u32[]{:S(2)}) copy-start(f32[16384]{0:T(1024)} %param.17) | copy-start | bytes 196612
  7.2 139.3 %all-reduce.15.cloned.1.call-start = ((), (), s32[]{:S(2)}) async-start(), calls=%async_computation | async-start | bytes 393216 | tf_op jit(solution)/shard_map/psum | solution.py:64
  14.2 19.3 %copy-start.3 = (f32[32,8,256]{2,1,0:T(8,128)S(1)}, f32[32,8,256]{2,1,0:T(8,128)}, u32[]{:S(2)}) copy-start(f32[32,8,256]{2,1,0:T(8,128)} %param.26) | copy-start | bytes 786436
  45.0 4.6 copy-start.1
  49.6 3.1 copy-start.9
  49.6 3.1 copy-start.6
  49.6 27.6 %copy-start.7 = (f32[2,3072]{1,0:T(2,128)S(1)}, f32[2,3072]{1,0:T(2,128)}, u32[]{:S(2)}) copy-start(f32[2,3072]{1,0:T(2,128)} %param.27) | copy-start | bytes 73732
  49.6 46.5 %copy-start.11 = (s32[8,256]{1,0:T(8,128)S(1)}, s32[8,256]{1,0:T(8,128)}, u32[]{:S(2)}) copy-start(s32[8,256]{1,0:T(8,128)} %param.16) | copy-start | bytes 24580
  49.6 46.6 %copy-start.8 = (f32[2,3072]{1,0:T(2,128)S(1)}, f32[2,3072]{1,0:T(2,128)}, u32[]{:S(2)}) copy-start(f32[2,3072]{1,0:T(2,128)} %param.25) | copy-start | bytes 73732
  49.6 78.8 %copy-start.5 = (f32[3072]{0:T(1024)S(1)}, f32[3072]{0:T(1024)}, u32[]{:S(2)}) copy-start(f32[3072]{0:T(1024)} %param.22) | copy-start | bytes 36868
  49.6 78.8 %copy-start.4 = (f32[3072]{0:T(1024)S(1)}, f32[3072]{0:T(1024)}, u32[]{:S(2)}) copy-start(f32[3072]{0:T(1024)} %param.20) | copy-start | bytes 36868
  49.6 78.8 %copy-start.10 = (f32[3072]{0:T(1024)S(1)}, f32[3072]{0:T(1024)}, u32[]{:S(2)}) copy-start(f32[3072]{0:T(1024)} %param.21) | copy-start | bytes 36868
  49.6 78.8 %copy-start.13 = (u32[32]{0:T(128)S(1)}, u32[32]{0:T(128)}, u32[]{:S(2)}) copy-start(u32[32]{0:T(128)} %constant.69) | copy-start | bytes 388
  49.6 80.0 %copy-start.12 = (f32[2]{0:T(128)S(1)}, f32[2]{0:T(128)}, u32[]{:S(2)}) copy-start(f32[2]{0:T(128)} %param.24) | copy-start | bytes 28
  49.7 98.7 %copy-start.2 = (f32[32,8,256]{2,1,0:T(8,128)S(1)}, f32[32,8,256]{2,1,0:T(8,128)}, u32[]{:S(2)}) copy-start(f32[32,8,256]{2,1,0:T(8,128)} %param.18) | copy-start | bytes 786436
  52.6 202.4 %all-reduce.17.cloned.1.call-start = ((), (), s32[]{:S(2)}) async-start(), calls=%async_computation.1 | async-start | bytes 393216 | tf_op jit(solution)/shard_map/psum | solution.py:64
  165.0 199.3 %all-reduce.19.cloned.1.call-start = ((), (), s32[]{:S(2)}) async-start(), calls=%async_computation.2 | async-start | bytes 393216 | tf_op jit(solution)/shard_map/psum | solution.py:64
  274.3 199.3 %all-reduce.21.cloned.1.call-start = ((), (), s32[]{:S(2)}) async-start(), calls=%async_computation.3 | async-start | bytes 393216 | tf_op jit(solution)/shard_map/psum | solution.py:64
Sparse Core Ops, SparseCore 0:
  52.8 93.6 all-reduce.14
  165.2 89.8 all-reduce.16
  274.5 89.8 all-reduce.18
  383.7 89.8 all-reduce.20
where the time goes:
time: 493 us; the launch traced here: 492 us
  waiting for transfers between devices  182 us (37%)
  blocking collectives  157 us (32%)
  matrix products  61 us (12%)
  local copies, waits for them, and re-layouts  45.1 us (9%)
  other arithmetic  24.1 us (5%)
  between operations  23 us (5%)
    psum x4, waiting for transfers between devices, body(): pulled = lax.psum(own_term.astype(jnp.bfloat16), 'ctg').astype(jnp.float32)  182 us
    psum x2, blocking collectives, body(): flow_sq = lax.psum(jnp.sum((dual_new - flow_dual) ** 2), 'ctg')  62.5 us
    dot_general x4, matrix products, body(): jnp.einsum('kmu,tu->tkm', masked, extended_half, preferred_element_type=j...  35.6 us
    unnamed x1, blocking collectives  31.2 us
    mul x2, local copies, waits for them, and re-layouts, mask_tiles(): return (blocks * gates).reshape(ctg_count, line_count, unit_count)  25.6 us
    dot_general x4, matrix products, body(): jnp.einsum('tkm,kmu->tu', dual_half, masked, preferred_element_type=jnp.f...  25.4 us
    all_gather x1, blocking collectives, body(): lax.all_gather(unit_cost, 'ctg', axis=0, tiled=True)  24.2 us
    all_gather x1, blocking collectives, body(): lax.all_gather(start_output, 'ctg', axis=0, tiled=True)  20.1 us
  transfers between devices with their start and end apart: 4, of which 4 were waited for; matrix products, arithmetic and copies ran while one was open for 3% of the time, Pallas kernels for 0%

commit v1 on v0

--- a/solution.py
+++ b/solution.py
@@ -61,7 +61,9 @@
         dual_step = step_size * weight
         dual_half = flow_dual.astype(jnp.bfloat16)
         own_term = jnp.einsum("tkm,kmu->tu", dual_half, masked, preferred_element_type=jnp.float32)
-        pulled = lax.psum(own_term.astype(jnp.bfloat16), "ctg").astype(jnp.float32)
+        pulled = jnp.sum(lax.all_gather(own_term.astype(jnp.bfloat16), "ctg"), axis=0).astype(
+            jnp.float32
+        )
         before = jnp.concatenate([zero_row, ramp_dual[:-1]], axis=0)
         gradient = (
             costs + pulled + ramp_on * (before - ramp_dual) + balance * balance_price[:, None]

time: 493 us -> 343 us (0.70)
  waiting for transfers between devices: 182 us -> 21 us
  other arithmetic: 24.1 us -> 30.5 us
    psum x4 -> x0, waiting for transfers between devices: 182 us -> none  [body(): pulled = lax.psum(own_term.astype(jnp.bfloat16), 'ctg').astype(jnp.float32)]
    all_gather x0 -> x4, waiting for transfers between devices: none -> 20.9 us  [body(): lax.all_gather(own_term.astype(jnp.bfloat16), 'ctg')]
    reduce_sum x0 -> x4, other arithmetic: none -> 9.96 us  [body(): jnp.sum(lax.all_gather(own_term.astype(jnp.bfloat16), 'ctg'), axis=0)]
  transfers between devices with their start and end apart: 4 -> 4, of which waited for: 4 -> 3; matrix products, arithmetic and copies ran while one was open for 3% -> 5% of each run, Pallas kernels for 0% -> 0%
where the time goes in v1:
time: 343 us; the launch traced here: 342 us
  blocking collectives  161 us (47%)
  matrix products  61 us (18%)
  local copies, waits for them, and re-layouts  45.1 us (13%)
  other arithmetic  30.5 us (9%)
  between operations  23.1 us (7%)
  waiting for transfers between devices  21 us (6%)
    psum x2, blocking collectives, body(): flow_sq = lax.psum(jnp.sum((dual_new - flow_dual) ** 2), 'ctg')  64.5 us
    dot_general x4, matrix products, body(): jnp.einsum('kmu,tu->tkm', masked, extended_half, preferred_element_type=j...  35.6 us
    unnamed x1, blocking collectives  31.3 us
    mul x2, local copies, waits for them, and re-layouts, mask_tiles(): return (blocks * gates).reshape(ctg_count, line_count, unit_count)  25.6 us
    dot_general x4, matrix products, body(): jnp.einsum('tkm,kmu->tu', dual_half, masked, preferred_element_type=jnp.f...  25.4 us
    all_gather x1, blocking collectives, body(): lax.all_gather(unit_cost, 'ctg', axis=0, tiled=True)  24.7 us
    all_gather x1, blocking collectives, body(): lax.all_gather(start_output, 'ctg', axis=0, tiled=True)  21.3 us
    all_gather x4, waiting for transfers between devices, body(): lax.all_gather(own_term.astype(jnp.bfloat16), 'ctg')  20.9 us
  transfers between devices with their start and end apart: 4, of which 3 were waited for; matrix products, arithmetic and copies ran while one was open for 5% of the time, Pallas kernels for 0%

profile of v1, /device:TPU:0, one launch (start us, length us, event | category | flops | bytes accessed | tf_op | source)
XLA Modules:
  0.0 341.7 jit_solution(2142437732403663585)
XLA Ops:
  7.2 0.7 convert_element_type.65
  7.9 6.3 %mul.232 = bf16[8,2,128,24,128]{4,3,2,1,0:T(8,128)(2,1)} broadcast(bf16[8,2,24]{2,1,0:T(2,128)(2,1)S(1)} %convert_element_type.65), dimensions={0,1,3} | broadcast | bytes 12583680 | tf_op jit(solution)/shard_map/mul | solution.py:14
  14.2 19.3 %mul.233 = bf16[8,256,3072]{2,1,0:T(8,128)(2,1)} reshape(bf16[8,2,128,24,128]{4,3,2,1,0:T(8,128)(2,1)} %mul.232) | data formatting | bytes 25165824 | tf_op jit(solution)/shard_map/mul | solution.py:14
  33.5 11.4 %mul.234 = bf16[8,256,3072]{2,1,0:T(8,128)(2,1)S(1)} multiply(bf16[8,256,3072]{2,1,0:T(8,128)(2,1)} %param.14, bf16[8,256,3072]{2,1,0:T(8,128)(2,1)} %mul.233) | non-fusion elementwise | flops 6291456 | bytes 37748736 | tf_op jit(solution)/shard_map/mul | solution.py:14
  45.0 4.6 %copy-done.2 = bf16[8,256,3072]{2,1,0:T(8,128)(2,1)} copy-done((bf16[8,256,3072]{2,1,0:T(8,128)(2,1)}, bf16[8,256,3072]{2,1,0:T(8,128)(2,1)S(1)}, u32[]{:S(2)}) %copy-start.2) | copy-done | bytes 12582936
  49.6 2.9 fusion.4
  52.7 24.7 %all-gather.5 = f32[16,2,3072]{2,1,0:T(2,128)S(1)} all-gather(f32[1,2,3072]{2,1,0:T(2,128)S(1)} %bitcast.72), channel_id=1, replica_groups=mesh['grp'=2,'ctg'=16] {'ctg'}, dimensions={0}, use_global_device_ids=true | all-gather | bytes 417792 | tf_op jit(solution)/shard_map/all_gather | solution.py:54
  77.4 0.3 reshape.44
  77.7 19.0 %all-gather.6 = f32[16,2,3072]{2,1,0:T(2,128)S(1)} all-gather(f32[1,2,3072]{2,1,0:T(2,128)S(1)} %bitcast.73), channel_id=1, replica_groups=mesh['grp'=2,'ctg'=16] {'ctg'}, dimensions={0}, use_global_device_ids=true | all-gather | bytes 417792 | tf_op jit(solution)/shard_map/all_gather | solution.py:55
  96.7 0.3 reshape.46
  97.0 21.3 %all-gather.4 = f32[16,2,3072]{2,1,0:T(2,128)S(1)} all-gather(f32[1,2,3072]{2,1,0:T(2,128)S(1)} %bitcast.74), channel_id=1, replica_groups=mesh['grp'=2,'ctg'=16] {'ctg'}, dimensions={0}, use_global_device_ids=true | all-gather | bytes 417792 | tf_op jit(solution)/shard_map/all_gather | solution.py:53
  118.3 0.3 reshape.42
  118.6 11.8 %gather_fusion = f32[2048]{0:T(1024)S(1)} fusion(f32[16384]{0:T(1024)S(1)} %copy-done, s32[2048]{0:T(1024)S(1)} %broadcast_clamp_fusion), kind=kCustom, calls=%fused_computation | custom fusion | bytes 24576 | tf_op jit(solution)/shard_map/gather | solution.py:41
  130.5 2.5 reduce_sum.192
  133.0 0.8 multiply_reduce_fusion.4
  133.8 0.2 fusion.34
  134.0 9.1 %multiply_reduce_fusion.8 = (f32[]{:T(128)}, f32[32,8,256]{2,0,1:T(8,128)S(1)}) fusion(f32[32,8,256]{2,1,0:T(8,128)S(1)} %copy-done.4, f32[8,256]{1,0:T(8,128)S(1)} %reshape.25, f32[32,8,256]{2,1,0:T(8,128)S(1)} %copy-done.3, bf16[8,256,3072]{2,1,0:T(8,128)(2,1)} %copy-done.2, f32[32,3072]{1,0:T(8,128)S(1)} %get-tuple-element.42), kind=kOutput, calls=%fused_computation.47 | convolution fusion | flops 403537920 | bytes 13770756 | tf_op jit(solution)/shard_map/kmu,tu->tkm/dot_general | solution.py:74
  143.1 7.5 %fusion = bf16[32,3072]{1,0:T(8,128)(2,1)} fusion(bf16[8,256,3072]{2,1,0:T(8,128)(2,1)} %copy-done.2, f32[32,8,256]{2,0,1:T(8,128)S(1)} %get-tuple-element.46, f32[32,8,256]{2,1,0:T(8,128)S(1)} %copy-done.3, f32[8,256]{1,0:T(8,128)S(1)} %reshape.25), kind=kOutput, calls=%fused_computation.5 | convolution fusion | flops 403275776 | bytes 13312000 | tf_op jit(solution)/shard_map/tkm,kmu->tu/dot_general | solution.py:63
  150.7 0.6 dynamic-slice
  152.0 0.2 dynamic-update-slice
  152.2 31.3 %all-reduce.9 = (f32[32]{0:T(128)S(1)}, f32[]{:T(128)}) all-reduce(f32[32]{0:T(128)S(1)} %dynamic-update-slice, f32[]{:T(128)} %get-tuple-element.45), channel_id=1, replica_groups=mesh['grp'=2,'ctg'=16] {'ctg'}, use_global_device_ids=true, to_apply=%add.8 | all-reduce | flops 33 | bytes 264
  183.6 0.8 multiply_reduce_fusion.5
  185.7 0.6 multiply_reduce_fusion.11
  187.7 5.7 %all-gather.14.cloned.1.call-done = bf16[512,3072]{1,0:T(8,128)(2,1)} async-done(((bf16[32,3072]{1,0:T(8,128)(2,1)}), bf16[512,3072]{1,0:T(8,128)(2,1)}) %all-gather.14.cloned.1.call-update) | async-done | bytes 3145744 | tf_op jit(solution)/shard_map/all_gather | solution.py:64
  193.4 2.5 reduce_sum.198
  195.9 0.8 multiply_reduce_fusion.2
  196.7 0.2 fusion.33
  196.9 9.1 %multiply_reduce_fusion.7 = (f32[]{:T(128)}, f32[32,8,256]{2,0,1:T(8,128)S(1)}) fusion(f32[32,8,256]{2,0,1:T(8,128)S(1)} %get-tuple-element.46, f32[]{:T(128)S(6)} %mul.251, f32[8,256]{1,0:T(8,128)S(1)} %reshape.25, f32[32,8,256]{2,1,0:T(8,128)S(1)} %copy-done.3, bf16[8,256,3072]{2,1,0:T(8,128)(2,1)} %copy-done.2, f32[32,3072]{1,0:T(8,128)S(1)} %get-tuple-element.36), kind=kOutput, calls=%fused_computation.44 | convolution fusion | flops 403865600 | bytes 13770760 | tf_op jit(solution)/shard_map/kmu,tu->tkm/dot_general | solution.py:74
  205.9 7.5 %fusion.1 = bf16[32,3072]{1,0:T(8,128)(2,1)} fusion(bf16[8,256,3072]{2,1,0:T(8,128)(2,1)} %copy-done.2, f32[32,8,256]{2,0,1:T(8,128)S(1)} %get-tuple-element.48, f32[]{:T(128)S(6)} %mul.251, f32[32,8,256]{2,1,0:T(8,128)S(1)} %copy-done.3, f32[8,256]{1,0:T(8,128)S(1)} %reshape.25), kind=kOutput, calls=%fused_computation.6 | convolution fusion | flops 403275776 | bytes 13312004 | tf_op jit(solution)/shard_map/tkm,kmu->tu/dot_general | solution.py:63
  213.5 32.2 %psum.22 = f32[]{:T(128)} all-reduce(f32[]{:T(128)} %get-tuple-element.47), channel_id=1, replica_groups=mesh['grp'=2,'ctg'=16] {'ctg'}, use_global_device_ids=true, to_apply=%region_9.10 | all-reduce | flops 1 | bytes 8 | tf_op jit(solution)/shard_map/psum | solution.py:82
  245.7 0.8 multiply_reduce_fusion.3
  247.8 0.6 multiply_reduce_fusion.10
  249.8 7.8 %all-gather.16.cloned.1.call-done = bf16[512,3072]{1,0:T(8,128)(2,1)} async-done(((bf16[32,3072]{1,0:T(8,128)(2,1)}), bf16[512,3072]{1,0:T(8,128)(2,1)}) %all-gather.16.cloned.1.call-update) | async-done | bytes 3145744 | tf_op jit(solution)/shard_map/all_gather | solution.py:64
  257.6 2.5 reduce_sum.204
  260.1 0.8 multiply_reduce_fusion
  260.9 0.2 fusion.32
  261.1 9.0 %multiply_reduce_fusion.6 = (f32[]{:T(128)}, f32[32,8,256]{2,0,1:T(8,128)S(1)}) fusion(f32[32,8,256]{2,0,1:T(8,128)S(1)} %get-tuple-element.48, f32[]{:T(128)S(6)} %mul.268, f32[]{:T(128)S(6)} %mul.251, f32[8,256]{1,0:T(8,128)S(1)} %reshape.25, f32[32,8,256]{2,1,0:T(8,128)S(1)} %copy-done.3, bf16[8,256,3072]{2,1,0:T(8,128)(2,1)} %copy-done.2, ...), kind=kOutput, calls=%fused_computation.41 | convolution fusion | flops 403865600 | bytes 13770764 | tf_op jit(solution)/shard_map/kmu,tu->tkm/dot_general | solution.py:74
  270.1 7.5 %fusion.2 = bf16[32,3072]{1,0:T(8,128)(2,1)} fusion(bf16[8,256,3072]{2,1,0:T(8,128)(2,1)} %copy-done.2, f32[32,8,256]{2,0,1:T(8,128)S(1)} %get-tuple-element.50, f32[]{:T(128)S(6)} %mul.268, f32[32,8,256]{2,1,0:T(8,128)S(1)} %copy-done.3, f32[8,256]{1,0:T(8,128)S(1)} %reshape.25), kind=kOutput, calls=%fused_computation.7 | convolution fusion | flops 403275776 | bytes 13312004 | tf_op jit(solution)/shard_map/tkm,kmu->tu/dot_general | solution.py:63
  277.7 32.4 %psum.23 = f32[]{:T(128)} all-reduce(f32[]{:T(128)} %get-tuple-element.49), channel_id=1, replica_groups=mesh['grp'=2,'ctg'=16] {'ctg'}, use_global_device_ids=true, to_apply=%region_16.17 | all-reduce | flops 1 | bytes 8 | tf_op jit(solution)/shard_map/psum | solution.py:82
  310.1 0.8 multiply_reduce_fusion.1
  312.2 0.6 multiply_reduce_fusion.9
  314.2 7.5 %all-gather.18.cloned.1.call-done = bf16[512,3072]{1,0:T(8,128)(2,1)} async-done(((bf16[32,3072]{1,0:T(8,128)(2,1)}), bf16[512,3072]{1,0:T(8,128)(2,1)}) %all-gather.18.cloned.1.call-update) | async-done | bytes 3145744 | tf_op jit(solution)/shard_map/all_gather | solution.py:64
  321.7 2.5 reduce_sum.210
  324.2 0.4 fusion.31
  324.6 8.4 %multiply_subtract_fusion.7 = f32[32,8,256]{2,0,1:T(8,128)S(1)} fusion(bf16[8,256,3072]{2,1,0:T(8,128)(2,1)} %copy-done.2, f32[32,8,256]{2,0,1:T(8,128)S(1)} %get-tuple-element.50, f32[32,3072]{1,0:T(8,128)S(1)} %get-tuple-element.19, f32[]{:T(128)S(6)} %mul.286, f32[]{:T(128)S(6)} %mul.268, f32[8,256]{1,0:T(8,128)S(1)} %reshape.25, ...), kind=kOutput, calls=%fused_computation.40 | convolution fusion | flops 403668992 | bytes 13770760 | tf_op jit(solution)/shard_map/kmu,tu->tkm/dot_general | solution.py:74
  333.0 0.9 copy.35
  333.9 0.6 dynamic_slice.11
  334.5 0.7 multiply_subtract_fusion.11
  (55 shorter events, 0.6 us)
Async XLA Ops:
  7.2 111.5 %copy-start = (f32[16384]{0:T(1024)S(1)}, f32[16384]{0:T(1024)}, u32[]{:S(2)}) copy-start(f32[16384]{0:T(1024)} %param.17) | copy-start | bytes 196612
  7.2 123.3 %all-gather.12.cloned.1.call-start = ((), (), s32[]{:S(2)}) async-start(), calls=%async_computation | async-start | bytes 3342336 | tf_op jit(solution)/shard_map/all_gather | solution.py:64
  14.2 19.3 %copy-start.4 = (f32[32,8,256]{2,1,0:T(8,128)S(1)}, f32[32,8,256]{2,1,0:T(8,128)}, u32[]{:S(2)}) copy-start(f32[32,8,256]{2,1,0:T(8,128)} %param.26) | copy-start | bytes 786436
  45.0 4.6 %copy-start.2 = (bf16[8,256,3072]{2,1,0:T(8,128)(2,1)}, bf16[8,256,3072]{2,1,0:T(8,128)(2,1)S(1)}, u32[]{:S(2)}) copy-start(bf16[8,256,3072]{2,1,0:T(8,128)(2,1)S(1)} %mul.234) | copy-start | bytes 37748740
  49.6 3.1 copy-start.10
  49.6 3.1 copy-start.7
  49.6 28.1 %copy-start.8 = (f32[2,3072]{1,0:T(2,128)S(1)}, f32[2,3072]{1,0:T(2,128)}, u32[]{:S(2)}) copy-start(f32[2,3072]{1,0:T(2,128)} %param.27) | copy-start | bytes 73732
  49.6 47.4 %copy-start.9 = (f32[2,3072]{1,0:T(2,128)S(1)}, f32[2,3072]{1,0:T(2,128)}, u32[]{:S(2)}) copy-start(f32[2,3072]{1,0:T(2,128)} %param.25) | copy-start | bytes 73732
  49.6 69.0 %copy-start.12 = (s32[8,256]{1,0:T(8,128)S(1)}, s32[8,256]{1,0:T(8,128)}, u32[]{:S(2)}) copy-start(s32[8,256]{1,0:T(8,128)} %param.16) | copy-start | bytes 24580
  49.6 80.8 %copy-start.5 = (f32[3072]{0:T(1024)S(1)}, f32[3072]{0:T(1024)}, u32[]{:S(2)}) copy-start(f32[3072]{0:T(1024)} %param.20) | copy-start | bytes 36868
  49.6 80.8 %copy-start.11 = (f32[3072]{0:T(1024)S(1)}, f32[3072]{0:T(1024)}, u32[]{:S(2)}) copy-start(f32[3072]{0:T(1024)} %param.21) | copy-start | bytes 36868
  52.6 81.4 %copy-start.3 = (f32[32,8,256]{2,1,0:T(8,128)S(1)}, f32[32,8,256]{2,1,0:T(8,128)}, u32[]{:S(2)}) copy-start(f32[32,8,256]{2,1,0:T(8,128)} %param.18) | copy-start | bytes 786436
  52.6 140.8 %all-gather.14.cloned.1.call-start = ((), (), s32[]{:S(2)}) async-start(), calls=%async_computation.1 | async-start | bytes 3342336 | tf_op jit(solution)/shard_map/all_gather | solution.py:64
  134.0 16.7 %copy-start.6 = (f32[3072]{0:T(1024)S(1)}, f32[3072]{0:T(1024)}, u32[]{:S(2)}) copy-start(f32[3072]{0:T(1024)} %param.22) | copy-start | bytes 36868
  134.0 16.8 %copy-start.14 = (u32[32]{0:T(128)S(1)}, u32[32]{0:T(128)}, u32[]{:S(2)}) copy-start(u32[32]{0:T(128)} %constant.74) | copy-start | bytes 388
  134.0 18.0 %copy-start.13 = (f32[2]{0:T(128)S(1)}, f32[2]{0:T(128)}, u32[]{:S(2)}) copy-start(f32[2]{0:T(128)} %param.24) | copy-start | bytes 28
  150.6 107.0 %all-gather.16.cloned.1.call-start = ((), (), s32[]{:S(2)}) async-start(), calls=%async_computation.2 | async-start | bytes 3342336 | tf_op jit(solution)/shard_map/all_gather | solution.py:64
  213.4 108.3 %all-gather.18.cloned.1.call-start = ((), (), s32[]{:S(2)}) async-start(), calls=%async_computation.3 | async-start | bytes 3342336 | tf_op jit(solution)/shard_map/all_gather | solution.py:64
  270.1 65.0 %copy-start.1 = (f32[16384]{0:T(1024)S(1)}, f32[16384]{0:T(1024)}, u32[]{:S(2)}) copy-start(f32[16384]{0:T(1024)} %param.17) | copy-start | bytes 196612
Sparse Core Ops, SparseCore 0:
  52.7 49.6 all-gather.11
  150.8 42.5 all-gather.13
  213.5 44.0 all-gather.15
  277.8 43.8 all-gather.17
